TPU v7x, 32 devices: a whole 2x2x4 slice. The times are simulated.
32 devices in a mesh: parts: 2 (over y), panel: 4 (over z), zone: 2 (over x), rhs: 2 (over core).
Axes of the slice: x: 2, y: 2, z: 4, core: 2. Of those that a mesh axis runs over, the one named last changes fastest.
Arguments:
- source: bfloat16 [4, 4096, 512], P(('parts', 'zone'), 'panel', 'rhs'), parts along dimension 0, may hold values from -6 to 6
- inverse: bfloat16 [4, 4096, 4096], P(('parts', 'zone'), 'panel'), parts along dimension 0, may hold values from -0.09375 to 0.09375
- coupling: bfloat16 [4, 4096, 4096], P(('parts', 'zone'), 'panel'), parts along dimension 0, may hold values from -0.078125 to 0.078125
Outputs:
- eliminated: bfloat16 [4, 4096, 512], P(('parts', 'zone'), 'panel', 'rhs'), parts along dimension 0
There are 2 independent parts, one for each index of `parts`. A program takes and returns all parts, laid end to end along the dimension named above; each array names one. Nothing has to cross between parts.
All inputs are finite; a program needn't handle non-finite values.
Results may differ from a plain program's by a relative error of at most 0.013.
Values may be sent and summed in bfloat16 or wider, within the bound.
No kernel may reach another device: no remote copies, remote signals or barrier semaphores. Data moves between devices by JAX's collectives and lax.ppermute only.
A program may use at most 64 MiB of HBM per device.

v0:
```python
import jax
import jax.numpy as jnp
from jax import lax
from jax.sharding import PartitionSpec as P


def from_behind(block, axis, distance):
    devices = range(lax.axis_size(axis))
    route = [(i - distance, i) for i in devices if i - distance in devices]
    return lax.ppermute(block, axis, route)


def local(source, inverse, coupling):
    inverse_block = inverse[0]
    coupling_block = coupling[0]
    local_rhs = source[0]
    row_count = local_rhs.shape[0]
    local_cols = local_rhs.shape[1]
    batch_count = 4
    group_cols = local_cols // batch_count
    zone_count = lax.axis_size("zone")
    zone_index = lax.axis_index("zone")
    total_steps = zone_count + batch_count - 1
    reduced = jnp.dot(
        inverse_block,
        lax.all_gather(local_rhs, "panel", axis=0, tiled=True),
        preferred_element_type=jnp.float32,
    )

    def advance(position, carried):
        previous, result = carried
        micro_index = position - zone_index
        is_live = jnp.logical_and(micro_index >= 0, micro_index < batch_count)
        clipped = jnp.clip(micro_index, 0, batch_count - 1)
        start_col = clipped * group_cols
        incoming = from_behind(previous, "zone", 1)
        initial = lax.dynamic_slice_in_dim(reduced, start_col, group_cols, 1)
        combined = initial - jnp.dot(
            coupling_block,
            lax.all_gather(incoming, "panel", axis=0, tiled=True),
            preferred_element_type=jnp.float32,
        )
        rounded = combined.astype(jnp.bfloat16)
        current = lax.dynamic_slice_in_dim(result, start_col, group_cols, 1)
        updated = lax.dynamic_update_slice_in_dim(
            result, jnp.where(is_live, rounded, current), start_col, 1
        )
        return (rounded, updated)

    starting = (
        jnp.zeros((row_count, group_cols), jnp.bfloat16),
        jnp.zeros((row_count, local_cols), jnp.bfloat16),
    )
    _, result = lax.fori_loop(0, total_steps, advance, starting)
    return result[None]


def solution(mesh):
    in_specs = (
        P(("parts", "zone"), "panel", "rhs"),
        P(("parts", "zone"), "panel", None),
        P(("parts", "zone"), "panel", None),
    )
    out_specs = P(("parts", "zone"), "panel", "rhs")
    return jax.shard_map(local, mesh=mesh, in_specs=in_specs, out_specs=out_specs, check_vma=False)
```

profile of v0, /device:TPU:0, one launch (start us, length us, event | category | flops | bytes accessed | tf_op | source)
XLA Modules:
  0.0 211.5 jit_solution(5797174708042044751)
XLA Ops:
  6.5 0.0 all-gather.3.cloned.1.call-start
  6.5 0.7 all-gather.3.cloned.1.call-update
  7.3 50.3 %all-gather.3.cloned.1.call-done = bf16[1,4096,256]{2,1,0:T(8,128)(2,1)} async-done(((bf16[1,1024,256]{2,1,0:T(8,128)(2,1)}), bf16[1,4096,256]{2,1,0:T(8,128)(2,1)}) %all-gather.3.cloned.1.call-update) | async-done | bytes 2097168 | tf_op jit(solution)/shard_map/all_gather | solution.py:26
  57.6 6.3 %fusion.1 = f32[1024,256]{0,1:T(8,128)S(1)} fusion(bf16[1,1024,4096]{2,1,0:T(8,128)(2,1)} %param.6, bf16[1,4096,256]{2,1,0:T(8,128)(2,1)} %all-gather.3.cloned.1.call-done), kind=kOutput, calls=%fused_computation.4 | convolution fusion | flops 2147483648 | bytes 11534336 | tf_op jit(solution)/shard_map/dot_general | solution.py:24
  64.0 0.1 broadcast_in_dim.10
  64.0 139.6 %while.16 = (s32[]{:T(128)}, bf16[1024,64]{0,1:T(8,128)(2,1)S(1)}, bf16[1024,256]{0,1:T(8,128)(2,1)S(1)}, s32[]{:T(128)}, f32[1024,256]{0,1:T(8,128)S(1)}, /*ind...) while((s32[]{:T(128)}, bf16[1024,64]{0,1:T(8,128)(2,1)S(1)}, ...), condition=%wide.region_1.2_spmd.clone, body=%wide.region_0.1_spmd.clone.sunk | while | flops 537133056 | bytes 11010323 | solution.py:54
  64.0 3.4 %collective-permute-start = (bf16[1024,64]{0,1:T(8,128)(2,1)S(1)}, bf16[1024,64]{0,1:T(8,128)(2,1)S(1)}, u32[]{:S(2)}, u32[]{:S(2)}) collective-permute-start(bf16[1024,64]{0,1:T(8,128)(2,1)S(1)} %broadcast_select_fusion.2), channel_id=1, source_target_pairs={{0,2},{1,3},{4,6},{5,7},{8,10},{9,11},{12,14},{13,15},{16,18},{17,... | collective-permute-start | bytes 393224 | tf_op jit(solution)/shard_map/while/body/eval_jaxpr/ppermute | solution.py:10
  67.5 2.7 %collective-permute-done = bf16[1024,64]{0,1:T(8,128)(2,1)S(1)} collective-permute-done((bf16[1024,64]{0,1:T(8,128)(2,1)S(1)}, bf16[1024,64]{0,1:T(8,128)(2,1)S(1)}, u32[]{:S(2)}, u32[]{:S(2)}) %collective-permute-start) | collective-permute-done | bytes 131104 | tf_op jit(solution)/shard_map/while/body/eval_jaxpr/ppermute | solution.py:10
  70.2 16.1 %all_gather.13 = bf16[4096,64]{0,1:T(8,128)(2,1)S(1)} all-gather(bf16[1024,64]{0,1:T(8,128)(2,1)S(1)} %collective-permute-done), channel_id=1, replica_groups=mesh['parts'=2,'panel'=4,'zone'=2,'rhs'=2] {'panel'}, dimensions={0}, use_global_device_ids=true | all-gather | bytes 655360 | tf_op jit(solution)/shard_map/while/body/eval_jaxpr/all_gather | solution.py:40
  86.2 6.0 %select_dynamic-update-slice_fusion.2 = (bf16[1024,256]{0,1:T(8,128)(2,1)S(1)}, bf16[1024,64]{0,1:T(8,128)(2,1)S(1)}) fusion(bf16[1024,256]{0,1:T(8,128)(2,1)S(1)} %get-tuple-element.211, s32[]{:T(128)S(6)} %select_n.35, pred[]{:T(512)S(6)} %and.10, bf16[1024,4096]{1,0:T(8,128)(2,1)} %get-tuple-element.226, bf16[4096,64]{0,1:T(8,128)(2,1)S(1)} %all_gather.13, ...), kind=kOutput, calls=%fused_computation.2.clone.1 | convolution fusion | flops 537067520 | bytes 9568261 | tf_op jit(solution)/shard_map/while/body/eval_jaxpr/dot_general | solution.py:38
  92.3 4.4 %collective-permute-start = (bf16[1024,64]{0,1:T(8,128)(2,1)S(1)}, bf16[1024,64]{0,1:T(8,128)(2,1)S(1)}, u32[]{:S(2)}, u32[]{:S(2)}) collective-permute-start(bf16[1024,64]{0,1:T(8,128)(2,1)S(1)} %broadcast_select_fusion.2), channel_id=1, source_target_pairs={{0,2},{1,3},{4,6},{5,7},{8,10},{9,11},{12,14},{13,15},{16,18},{17,... | collective-permute-start | bytes 393224 | tf_op jit(solution)/shard_map/while/body/eval_jaxpr/ppermute | solution.py:10
  96.7 2.5 %collective-permute-done = bf16[1024,64]{0,1:T(8,128)(2,1)S(1)} collective-permute-done((bf16[1024,64]{0,1:T(8,128)(2,1)S(1)}, bf16[1024,64]{0,1:T(8,128)(2,1)S(1)}, u32[]{:S(2)}, u32[]{:S(2)}) %collective-permute-start) | collective-permute-done | bytes 131104 | tf_op jit(solution)/shard_map/while/body/eval_jaxpr/ppermute | solution.py:10
  99.2 15.8 %all_gather.13 = bf16[4096,64]{0,1:T(8,128)(2,1)S(1)} all-gather(bf16[1024,64]{0,1:T(8,128)(2,1)S(1)} %collective-permute-done), channel_id=1, replica_groups=mesh['parts'=2,'panel'=4,'zone'=2,'rhs'=2] {'panel'}, dimensions={0}, use_global_device_ids=true | all-gather | bytes 655360 | tf_op jit(solution)/shard_map/while/body/eval_jaxpr/all_gather | solution.py:40
  115.0 6.0 %select_dynamic-update-slice_fusion.2 = (bf16[1024,256]{0,1:T(8,128)(2,1)S(1)}, bf16[1024,64]{0,1:T(8,128)(2,1)S(1)}) fusion(bf16[1024,256]{0,1:T(8,128)(2,1)S(1)} %get-tuple-element.211, s32[]{:T(128)S(6)} %select_n.35, pred[]{:T(512)S(6)} %and.10, bf16[1024,4096]{1,0:T(8,128)(2,1)} %get-tuple-element.226, bf16[4096,64]{0,1:T(8,128)(2,1)S(1)} %all_gather.13, ...), kind=kOutput, calls=%fused_computation.2.clone.1 | convolution fusion | flops 537067520 | bytes 9568261 | tf_op jit(solution)/shard_map/while/body/eval_jaxpr/dot_general | solution.py:38
  121.1 4.0 %collective-permute-start = (bf16[1024,64]{0,1:T(8,128)(2,1)S(1)}, bf16[1024,64]{0,1:T(8,128)(2,1)S(1)}, u32[]{:S(2)}, u32[]{:S(2)}) collective-permute-start(bf16[1024,64]{0,1:T(8,128)(2,1)S(1)} %broadcast_select_fusion.2), channel_id=1, source_target_pairs={{0,2},{1,3},{4,6},{5,7},{8,10},{9,11},{12,14},{13,15},{16,18},{17,... | collective-permute-start | bytes 393224 | tf_op jit(solution)/shard_map/while/body/eval_jaxpr/ppermute | solution.py:10
  125.1 2.5 %collective-permute-done = bf16[1024,64]{0,1:T(8,128)(2,1)S(1)} collective-permute-done((bf16[1024,64]{0,1:T(8,128)(2,1)S(1)}, bf16[1024,64]{0,1:T(8,128)(2,1)S(1)}, u32[]{:S(2)}, u32[]{:S(2)}) %collective-permute-start) | collective-permute-done | bytes 131104 | tf_op jit(solution)/shard_map/while/body/eval_jaxpr/ppermute | solution.py:10
  127.6 14.7 %all_gather.13 = bf16[4096,64]{0,1:T(8,128)(2,1)S(1)} all-gather(bf16[1024,64]{0,1:T(8,128)(2,1)S(1)} %collective-permute-done), channel_id=1, replica_groups=mesh['parts'=2,'panel'=4,'zone'=2,'rhs'=2] {'panel'}, dimensions={0}, use_global_device_ids=true | all-gather | bytes 655360 | tf_op jit(solution)/shard_map/while/body/eval_jaxpr/all_gather | solution.py:40
  142.4 6.0 %select_dynamic-update-slice_fusion.2 = (bf16[1024,256]{0,1:T(8,128)(2,1)S(1)}, bf16[1024,64]{0,1:T(8,128)(2,1)S(1)}) fusion(bf16[1024,256]{0,1:T(8,128)(2,1)S(1)} %get-tuple-element.211, s32[]{:T(128)S(6)} %select_n.35, pred[]{:T(512)S(6)} %and.10, bf16[1024,4096]{1,0:T(8,128)(2,1)} %get-tuple-element.226, bf16[4096,64]{0,1:T(8,128)(2,1)S(1)} %all_gather.13, ...), kind=kOutput, calls=%fused_computation.2.clone.1 | convolution fusion | flops 537067520 | bytes 9568261 | tf_op jit(solution)/shard_map/while/body/eval_jaxpr/dot_general | solution.py:38
  148.4 4.4 %collective-permute-start = (bf16[1024,64]{0,1:T(8,128)(2,1)S(1)}, bf16[1024,64]{0,1:T(8,128)(2,1)S(1)}, u32[]{:S(2)}, u32[]{:S(2)}) collective-permute-start(bf16[1024,64]{0,1:T(8,128)(2,1)S(1)} %broadcast_select_fusion.2), channel_id=1, source_target_pairs={{0,2},{1,3},{4,6},{5,7},{8,10},{9,11},{12,14},{13,15},{16,18},{17,... | collective-permute-start | bytes 393224 | tf_op jit(solution)/shard_map/while/body/eval_jaxpr/ppermute | solution.py:10
  152.8 2.5 %collective-permute-done = bf16[1024,64]{0,1:T(8,128)(2,1)S(1)} collective-permute-done((bf16[1024,64]{0,1:T(8,128)(2,1)S(1)}, bf16[1024,64]{0,1:T(8,128)(2,1)S(1)}, u32[]{:S(2)}, u32[]{:S(2)}) %collective-permute-start) | collective-permute-done | bytes 131104 | tf_op jit(solution)/shard_map/while/body/eval_jaxpr/ppermute | solution.py:10
  155.3 14.7 %all_gather.13 = bf16[4096,64]{0,1:T(8,128)(2,1)S(1)} all-gather(bf16[1024,64]{0,1:T(8,128)(2,1)S(1)} %collective-permute-done), channel_id=1, replica_groups=mesh['parts'=2,'panel'=4,'zone'=2,'rhs'=2] {'panel'}, dimensions={0}, use_global_device_ids=true | all-gather | bytes 655360 | tf_op jit(solution)/shard_map/while/body/eval_jaxpr/all_gather | solution.py:40
  170.0 6.0 %select_dynamic-update-slice_fusion.2 = (bf16[1024,256]{0,1:T(8,128)(2,1)S(1)}, bf16[1024,64]{0,1:T(8,128)(2,1)S(1)}) fusion(bf16[1024,256]{0,1:T(8,128)(2,1)S(1)} %get-tuple-element.211, s32[]{:T(128)S(6)} %select_n.35, pred[]{:T(512)S(6)} %and.10, bf16[1024,4096]{1,0:T(8,128)(2,1)} %get-tuple-element.226, bf16[4096,64]{0,1:T(8,128)(2,1)S(1)} %all_gather.13, ...), kind=kOutput, calls=%fused_computation.2.clone.1 | convolution fusion | flops 537067520 | bytes 9568261 | tf_op jit(solution)/shard_map/while/body/eval_jaxpr/dot_general | solution.py:38
  176.1 4.4 %collective-permute-start = (bf16[1024,64]{0,1:T(8,128)(2,1)S(1)}, bf16[1024,64]{0,1:T(8,128)(2,1)S(1)}, u32[]{:S(2)}, u32[]{:S(2)}) collective-permute-start(bf16[1024,64]{0,1:T(8,128)(2,1)S(1)} %broadcast_select_fusion.2), channel_id=1, source_target_pairs={{0,2},{1,3},{4,6},{5,7},{8,10},{9,11},{12,14},{13,15},{16,18},{17,... | collective-permute-start | bytes 393224 | tf_op jit(solution)/shard_map/while/body/eval_jaxpr/ppermute | solution.py:10
  180.5 2.5 %collective-permute-done = bf16[1024,64]{0,1:T(8,128)(2,1)S(1)} collective-permute-done((bf16[1024,64]{0,1:T(8,128)(2,1)S(1)}, bf16[1024,64]{0,1:T(8,128)(2,1)S(1)}, u32[]{:S(2)}, u32[]{:S(2)}) %collective-permute-start) | collective-permute-done | bytes 131104 | tf_op jit(solution)/shard_map/while/body/eval_jaxpr/ppermute | solution.py:10
  182.9 14.6 %all_gather.13 = bf16[4096,64]{0,1:T(8,128)(2,1)S(1)} all-gather(bf16[1024,64]{0,1:T(8,128)(2,1)S(1)} %collective-permute-done), channel_id=1, replica_groups=mesh['parts'=2,'panel'=4,'zone'=2,'rhs'=2] {'panel'}, dimensions={0}, use_global_device_ids=true | all-gather | bytes 655360 | tf_op jit(solution)/shard_map/while/body/eval_jaxpr/all_gather | solution.py:40
  197.6 6.0 %select_dynamic-update-slice_fusion.2 = (bf16[1024,256]{0,1:T(8,128)(2,1)S(1)}, bf16[1024,64]{0,1:T(8,128)(2,1)S(1)}) fusion(bf16[1024,256]{0,1:T(8,128)(2,1)S(1)} %get-tuple-element.211, s32[]{:T(128)S(6)} %select_n.35, pred[]{:T(512)S(6)} %and.10, bf16[1024,4096]{1,0:T(8,128)(2,1)} %get-tuple-element.226, bf16[4096,64]{0,1:T(8,128)(2,1)S(1)} %all_gather.13, ...), kind=kOutput, calls=%fused_computation.2.clone.1 | convolution fusion | flops 537067520 | bytes 9568261 | tf_op jit(solution)/shard_map/while/body/eval_jaxpr/dot_general | solution.py:38
  203.6 1.0 copy.5
  (6 shorter events, 0.1 us)
Async XLA Ops:
  6.5 51.1 %all-gather.3.cloned.1.call-start = ((), (), s32[]{:S(2)}) async-start(), calls=%async_computation | async-start | bytes 2621440 | tf_op jit(solution)/shard_map/all_gather | solution.py:26
  64.0 6.1 %collective-permute-start = (bf16[1024,64]{0,1:T(8,128)(2,1)S(1)}, bf16[1024,64]{0,1:T(8,128)(2,1)S(1)}, u32[]{:S(2)}, u32[]{:S(2)}) collective-permute-start(bf16[1024,64]{0,1:T(8,128)(2,1)S(1)} %broadcast_select_fusion.2), channel_id=1, source_target_pairs={{0,2},{1,3},{4,6},{5,7},{8,10},{9,11},{12,14},{13,15},{16,18},{17,... | collective-permute-start | bytes 393224 | tf_op jit(solution)/shard_map/while/body/eval_jaxpr/ppermute | solution.py:10
  92.3 6.9 %collective-permute-start = (bf16[1024,64]{0,1:T(8,128)(2,1)S(1)}, bf16[1024,64]{0,1:T(8,128)(2,1)S(1)}, u32[]{:S(2)}, u32[]{:S(2)}) collective-permute-start(bf16[1024,64]{0,1:T(8,128)(2,1)S(1)} %broadcast_select_fusion.2), channel_id=1, source_target_pairs={{0,2},{1,3},{4,6},{5,7},{8,10},{9,11},{12,14},{13,15},{16,18},{17,... | collective-permute-start | bytes 393224 | tf_op jit(solution)/shard_map/while/body/eval_jaxpr/ppermute | solution.py:10
  121.1 6.6 %collective-permute-start = (bf16[1024,64]{0,1:T(8,128)(2,1)S(1)}, bf16[1024,64]{0,1:T(8,128)(2,1)S(1)}, u32[]{:S(2)}, u32[]{:S(2)}) collective-permute-start(bf16[1024,64]{0,1:T(8,128)(2,1)S(1)} %broadcast_select_fusion.2), channel_id=1, source_target_pairs={{0,2},{1,3},{4,6},{5,7},{8,10},{9,11},{12,14},{13,15},{16,18},{17,... | collective-permute-start | bytes 393224 | tf_op jit(solution)/shard_map/while/body/eval_jaxpr/ppermute | solution.py:10
  148.4 6.9 %collective-permute-start = (bf16[1024,64]{0,1:T(8,128)(2,1)S(1)}, bf16[1024,64]{0,1:T(8,128)(2,1)S(1)}, u32[]{:S(2)}, u32[]{:S(2)}) collective-permute-start(bf16[1024,64]{0,1:T(8,128)(2,1)S(1)} %broadcast_select_fusion.2), channel_id=1, source_target_pairs={{0,2},{1,3},{4,6},{5,7},{8,10},{9,11},{12,14},{13,15},{16,18},{17,... | collective-permute-start | bytes 393224 | tf_op jit(solution)/shard_map/while/body/eval_jaxpr/ppermute | solution.py:10
  176.1 6.9 %collective-permute-start = (bf16[1024,64]{0,1:T(8,128)(2,1)S(1)}, bf16[1024,64]{0,1:T(8,128)(2,1)S(1)}, u32[]{:S(2)}, u32[]{:S(2)}) collective-permute-start(bf16[1024,64]{0,1:T(8,128)(2,1)S(1)} %broadcast_select_fusion.2), channel_id=1, source_target_pairs={{0,2},{1,3},{4,6},{5,7},{8,10},{9,11},{12,14},{13,15},{16,18},{17,... | collective-permute-start | bytes 393224 | tf_op jit(solution)/shard_map/while/body/eval_jaxpr/ppermute | solution.py:10
Sparse Core Ops, SparseCore 0:
  8.9 48.6 all-gather.2
where the time goes:
time: 212 us; the launch traced here: 211 us
  blocking collectives  75.9 us (36%)
  waiting for transfers between devices  63.7 us (30%)
  matrix products  36.6 us (17%)
  starting transfers between devices  20.5 us (10%)
  between operations  13.4 us (6%)
    all_gather x5, blocking collectives, advance(): lax.all_gather(incoming, 'panel', axis=0, tiled=True)  75.9 us
    all_gather x1, waiting for transfers between devices, local(): lax.all_gather(local_rhs, 'panel', axis=0, tiled=True)  50.3 us
    dot_general x5, matrix products, advance(): jnp.dot(coupling_block, lax.all_gather(incoming, 'panel', axis=0, tiled=T...  30.2 us
    ppermute x5, starting transfers between devices, from_behind(): return lax.ppermute(block, axis, route)  20.5 us
    ppermute x5, waiting for transfers between devices, from_behind(): return lax.ppermute(block, axis, route)  12.6 us
    dot_general x1, matrix products, local(): jnp.dot(inverse_block, lax.all_gather(local_rhs, 'panel', axis=0, tiled=T...  6.34 us
  transfers between devices with their start and end apart: 6, of which 6 were waited for; matrix products, arithmetic and copies ran while one was open for 0% of the time, Pallas kernels for 0%

commit v1 on v0

--- a/solution.py
+++ b/solution.py
@@ -2,6 +2,16 @@
 import jax.numpy as jnp
 from jax import lax
 from jax.sharding import PartitionSpec as P
+
+
+def gather_around(x, axis, dim):
+    ways, here, lap = (lax.axis_size(axis), lax.axis_index(axis), x.shape[dim])
+    shape = [n * ways if d == dim else n for d, n in enumerate(x.shape)]
+    full = lax.dynamic_update_slice_in_dim(jnp.zeros(shape, x.dtype), x, here * lap, axis=dim)
+    for far in range(1, ways):
+        x = lax.ppermute(x, axis, [(d, (d + 1) % ways) for d in range(ways)])
+        full = lax.dynamic_update_slice_in_dim(full, x, (here - far) % ways * lap, axis=dim)
+    return full
 
 
 def from_behind(block, axis, distance):
@@ -22,9 +32,7 @@
     zone_index = lax.axis_index("zone")
     total_steps = zone_count + batch_count - 1
     reduced = jnp.dot(
-        inverse_block,
-        lax.all_gather(local_rhs, "panel", axis=0, tiled=True),
-        preferred_element_type=jnp.float32,
+        inverse_block, gather_around(local_rhs, "panel", 0), preferred_element_type=jnp.float32
     )
 
     def advance(position, carried):

time: 212 us -> 191 us (0.901)
  between operations: 13.4 us -> 0.07 us
  waiting for transfers between devices: 63.7 us -> 55.2 us
  starting transfers between devices: 20.5 us -> 23.6 us
  blocking collectives: 75.9 us -> 73.6 us
    all_gather x1 -> x0, waiting for transfers between devices: 50.3 us -> none  [local(): lax.all_gather(local_rhs, 'panel', axis=0, tiled=True)]
    ppermute x0 -> x3, waiting for transfers between devices: none -> 42.8 us  [gather_around(): x = lax.ppermute(x, axis, [(d, (d + 1) % ways) for d in range(ways)])]
    ppermute x0 -> x3, starting transfers between devices: none -> 3.03 us  [gather_around(): x = lax.ppermute(x, axis, [(d, (d + 1) % ways) for d in range(ways)])]
    all_gather x5, blocking collectives: 75.9 us -> 73.6 us  [advance(): lax.all_gather(incoming, 'panel', axis=0, tiled=True)]
  transfers between devices with their start and end apart: 6 -> 8, of which waited for: 6 -> 8; matrix products, arithmetic and copies ran while one was open for 0% -> 0% of each run, Pallas kernels for 0% -> 0%
where the time goes in v1:
time: 191 us; the launch traced here: 190 us
  blocking collectives  73.6 us (39%)
  waiting for transfers between devices  55.2 us (29%)
  matrix products  36 us (19%)
  starting transfers between devices  23.6 us (12%)
    all_gather x5, blocking collectives, advance(): lax.all_gather(incoming, 'panel', axis=0, tiled=True)  73.6 us
    ppermute x3, waiting for transfers between devices, gather_around(): x = lax.ppermute(x, axis, [(d, (d + 1) % ways) for d in range(ways)])  42.8 us
    dot_general x5, matrix products, advance(): jnp.dot(coupling_block, lax.all_gather(incoming, 'panel', axis=0, tiled=T...  30.2 us
    ppermute x5, starting transfers between devices, from_behind(): return lax.ppermute(block, axis, route)  20.6 us
    ppermute x5, waiting for transfers between devices, from_behind(): return lax.ppermute(block, axis, route)  12.4 us
    dot_general x1, matrix products, local(): jnp.dot(inverse_block, gather_around(local_rhs, 'panel', 0), preferred_el...  5.76 us
  transfers between devices with their start and end apart: 8, of which 8 were waited for; matrix products, arithmetic and copies ran while one was open for 0% of the time, Pallas kernels for 0%

profile of v1, /device:TPU:0, one launch (start us, length us, event | category | flops | bytes accessed | tf_op | source)
XLA Modules:
  0.0 190.1 jit_solution(9714795842926822278)
XLA Ops:
  0.0 3.0 %collective-permute-start.1 = (bf16[1024,256]{1,0:T(8,128)(2,1)}, bf16[1024,256]{1,0:T(8,128)(2,1)S(1)}, u32[]{:S(2)}, u32[]{:S(2)}) collective-permute-start(bf16[1024,256]{1,0:T(8,128)(2,1)} %bitcast.19), channel_id=1, source_target_pairs={{0,4},{4,8},{8,12},{12,0},{1,5},{5,9},{9,13},{13,1},{2,6},{6,10},{... | collective-permute-start | bytes 1572872 | tf_op jit(solution)/shard_map/ppermute | solution.py:12
  3.0 14.2 %collective-permute-done.1 = bf16[1024,256]{1,0:T(8,128)(2,1)S(1)} collective-permute-done((bf16[1024,256]{1,0:T(8,128)(2,1)}, bf16[1024,256]{1,0:T(8,128)(2,1)S(1)}, u32[]{:S(2)}, u32[]{:S(2)}) %collective-permute-start.1) | collective-permute-done | bytes 524320 | tf_op jit(solution)/shard_map/ppermute | solution.py:12
  17.3 0.0 collective-permute-start.2
  17.3 14.9 %collective-permute-done.2 = bf16[1024,256]{1,0:T(8,128)(2,1)S(1)} collective-permute-done((bf16[1024,256]{1,0:T(8,128)(2,1)S(1)}, bf16[1024,256]{1,0:T(8,128)(2,1)S(1)}, u32[]{:S(2)}, u32[]{:S(2)}) %collective-permute-start.2) | collective-permute-done | bytes 524320 | tf_op jit(solution)/shard_map/ppermute | solution.py:12
  32.2 0.0 collective-permute-start.3
  32.2 0.1 broadcast_in_dim.14
  32.3 0.0 copy-done
  32.5 13.7 %collective-permute-done.3 = bf16[1024,256]{1,0:T(8,128)(2,1)S(1)} collective-permute-done((bf16[1024,256]{1,0:T(8,128)(2,1)S(1)}, bf16[1024,256]{1,0:T(8,128)(2,1)S(1)}, u32[]{:S(2)}, u32[]{:S(2)}) %collective-permute-start.3) | collective-permute-done | bytes 524320 | tf_op jit(solution)/shard_map/ppermute | solution.py:12
  46.2 5.8 %fusion.3 = f32[1024,256]{0,1:T(8,128)S(1)} fusion(bf16[4096,256]{1,0:T(8,128)(2,1)S(1)} %constant_dynamic-update-slice_fusion, bf16[1,1024,4096]{2,1,0:T(8,128)(2,1)} %param.6), kind=kOutput, calls=%fused_computation.6 | convolution fusion | flops 2147483648 | bytes 11534336 | tf_op jit(solution)/shard_map/dot_general | solution.py:34
  52.0 0.1 broadcast_in_dim.13
  52.0 137.1 %while.16 = (s32[]{:T(128)}, bf16[1024,64]{0,1:T(8,128)(2,1)S(1)}, bf16[1024,256]{0,1:T(8,128)(2,1)S(1)}, s32[]{:T(128)}, f32[1024,256]{0,1:T(8,128)S(1)}, /*ind...) while((s32[]{:T(128)}, bf16[1024,64]{0,1:T(8,128)(2,1)S(1)}, ...), condition=%wide.region_1.2_spmd.clone, body=%wide.region_0.1_spmd.clone.sunk | while | flops 537133056 | bytes 11010323 | solution.py:62
  52.1 3.1 %collective-permute-start = (bf16[1024,64]{0,1:T(8,128)(2,1)S(1)}, bf16[1024,64]{0,1:T(8,128)(2,1)S(1)}, u32[]{:S(2)}, u32[]{:S(2)}) collective-permute-start(bf16[1024,64]{0,1:T(8,128)(2,1)S(1)} %broadcast_select_fusion.2), channel_id=1, source_target_pairs={{0,2},{1,3},{4,6},{5,7},{8,10},{9,11},{12,14},{13,15},{16,18},{17,... | collective-permute-start | bytes 393224 | tf_op jit(solution)/shard_map/while/body/eval_jaxpr/ppermute | solution.py:20
  55.1 2.5 %collective-permute-done = bf16[1024,64]{0,1:T(8,128)(2,1)S(1)} collective-permute-done((bf16[1024,64]{0,1:T(8,128)(2,1)S(1)}, bf16[1024,64]{0,1:T(8,128)(2,1)S(1)}, u32[]{:S(2)}, u32[]{:S(2)}) %collective-permute-start) | collective-permute-done | bytes 131104 | tf_op jit(solution)/shard_map/while/body/eval_jaxpr/ppermute | solution.py:20
  57.6 14.8 %all_gather.9 = bf16[4096,64]{0,1:T(8,128)(2,1)S(1)} all-gather(bf16[1024,64]{0,1:T(8,128)(2,1)S(1)} %collective-permute-done), channel_id=1, replica_groups=mesh['parts'=2,'panel'=4,'zone'=2,'rhs'=2] {'panel'}, dimensions={0}, use_global_device_ids=true | all-gather | bytes 655360 | tf_op jit(solution)/shard_map/while/body/eval_jaxpr/all_gather | solution.py:48
  72.4 6.0 %select_dynamic-update-slice_fusion.2 = (bf16[1024,256]{0,1:T(8,128)(2,1)S(1)}, bf16[1024,64]{0,1:T(8,128)(2,1)S(1)}) fusion(bf16[1024,256]{0,1:T(8,128)(2,1)S(1)} %get-tuple-element.205, s32[]{:T(128)S(6)} %select_n.69, pred[]{:T(512)S(6)} %and.27, bf16[1024,4096]{1,0:T(8,128)(2,1)} %get-tuple-element.220, bf16[4096,64]{0,1:T(8,128)(2,1)S(1)} %all_gather.9, ...), kind=kOutput, calls=%fused_computation.2.clone.1 | convolution fusion | flops 537067520 | bytes 9568261 | tf_op jit(solution)/shard_map/while/body/eval_jaxpr/dot_general | solution.py:46
  78.5 4.4 %collective-permute-start = (bf16[1024,64]{0,1:T(8,128)(2,1)S(1)}, bf16[1024,64]{0,1:T(8,128)(2,1)S(1)}, u32[]{:S(2)}, u32[]{:S(2)}) collective-permute-start(bf16[1024,64]{0,1:T(8,128)(2,1)S(1)} %broadcast_select_fusion.2), channel_id=1, source_target_pairs={{0,2},{1,3},{4,6},{5,7},{8,10},{9,11},{12,14},{13,15},{16,18},{17,... | collective-permute-start | bytes 393224 | tf_op jit(solution)/shard_map/while/body/eval_jaxpr/ppermute | solution.py:20
  83.0 2.5 %collective-permute-done = bf16[1024,64]{0,1:T(8,128)(2,1)S(1)} collective-permute-done((bf16[1024,64]{0,1:T(8,128)(2,1)S(1)}, bf16[1024,64]{0,1:T(8,128)(2,1)S(1)}, u32[]{:S(2)}, u32[]{:S(2)}) %collective-permute-start) | collective-permute-done | bytes 131104 | tf_op jit(solution)/shard_map/while/body/eval_jaxpr/ppermute | solution.py:20
  85.4 14.6 %all_gather.9 = bf16[4096,64]{0,1:T(8,128)(2,1)S(1)} all-gather(bf16[1024,64]{0,1:T(8,128)(2,1)S(1)} %collective-permute-done), channel_id=1, replica_groups=mesh['parts'=2,'panel'=4,'zone'=2,'rhs'=2] {'panel'}, dimensions={0}, use_global_device_ids=true | all-gather | bytes 655360 | tf_op jit(solution)/shard_map/while/body/eval_jaxpr/all_gather | solution.py:48
  100.1 6.0 %select_dynamic-update-slice_fusion.2 = (bf16[1024,256]{0,1:T(8,128)(2,1)S(1)}, bf16[1024,64]{0,1:T(8,128)(2,1)S(1)}) fusion(bf16[1024,256]{0,1:T(8,128)(2,1)S(1)} %get-tuple-element.205, s32[]{:T(128)S(6)} %select_n.69, pred[]{:T(512)S(6)} %and.27, bf16[1024,4096]{1,0:T(8,128)(2,1)} %get-tuple-element.220, bf16[4096,64]{0,1:T(8,128)(2,1)S(1)} %all_gather.9, ...), kind=kOutput, calls=%fused_computation.2.clone.1 | convolution fusion | flops 537067520 | bytes 9568261 | tf_op jit(solution)/shard_map/while/body/eval_jaxpr/dot_general | solution.py:46
  106.2 4.4 %collective-permute-start = (bf16[1024,64]{0,1:T(8,128)(2,1)S(1)}, bf16[1024,64]{0,1:T(8,128)(2,1)S(1)}, u32[]{:S(2)}, u32[]{:S(2)}) collective-permute-start(bf16[1024,64]{0,1:T(8,128)(2,1)S(1)} %broadcast_select_fusion.2), channel_id=1, source_target_pairs={{0,2},{1,3},{4,6},{5,7},{8,10},{9,11},{12,14},{13,15},{16,18},{17,... | collective-permute-start | bytes 393224 | tf_op jit(solution)/shard_map/while/body/eval_jaxpr/ppermute | solution.py:20
  110.6 2.5 %collective-permute-done = bf16[1024,64]{0,1:T(8,128)(2,1)S(1)} collective-permute-done((bf16[1024,64]{0,1:T(8,128)(2,1)S(1)}, bf16[1024,64]{0,1:T(8,128)(2,1)S(1)}, u32[]{:S(2)}, u32[]{:S(2)}) %collective-permute-start) | collective-permute-done | bytes 131104 | tf_op jit(solution)/shard_map/while/body/eval_jaxpr/ppermute | solution.py:20
  113.0 14.6 %all_gather.9 = bf16[4096,64]{0,1:T(8,128)(2,1)S(1)} all-gather(bf16[1024,64]{0,1:T(8,128)(2,1)S(1)} %collective-permute-done), channel_id=1, replica_groups=mesh['parts'=2,'panel'=4,'zone'=2,'rhs'=2] {'panel'}, dimensions={0}, use_global_device_ids=true | all-gather | bytes 655360 | tf_op jit(solution)/shard_map/while/body/eval_jaxpr/all_gather | solution.py:48
  127.7 6.0 %select_dynamic-update-slice_fusion.2 = (bf16[1024,256]{0,1:T(8,128)(2,1)S(1)}, bf16[1024,64]{0,1:T(8,128)(2,1)S(1)}) fusion(bf16[1024,256]{0,1:T(8,128)(2,1)S(1)} %get-tuple-element.205, s32[]{:T(128)S(6)} %select_n.69, pred[]{:T(512)S(6)} %and.27, bf16[1024,4096]{1,0:T(8,128)(2,1)} %get-tuple-element.220, bf16[4096,64]{0,1:T(8,128)(2,1)S(1)} %all_gather.9, ...), kind=kOutput, calls=%fused_computation.2.clone.1 | convolution fusion | flops 537067520 | bytes 9568261 | tf_op jit(solution)/shard_map/while/body/eval_jaxpr/dot_general | solution.py:46
  133.8 4.4 %collective-permute-start = (bf16[1024,64]{0,1:T(8,128)(2,1)S(1)}, bf16[1024,64]{0,1:T(8,128)(2,1)S(1)}, u32[]{:S(2)}, u32[]{:S(2)}) collective-permute-start(bf16[1024,64]{0,1:T(8,128)(2,1)S(1)} %broadcast_select_fusion.2), channel_id=1, source_target_pairs={{0,2},{1,3},{4,6},{5,7},{8,10},{9,11},{12,14},{13,15},{16,18},{17,... | collective-permute-start | bytes 393224 | tf_op jit(solution)/shard_map/while/body/eval_jaxpr/ppermute | solution.py:20
  138.2 2.5 %collective-permute-done = bf16[1024,64]{0,1:T(8,128)(2,1)S(1)} collective-permute-done((bf16[1024,64]{0,1:T(8,128)(2,1)S(1)}, bf16[1024,64]{0,1:T(8,128)(2,1)S(1)}, u32[]{:S(2)}, u32[]{:S(2)}) %collective-permute-start) | collective-permute-done | bytes 131104 | tf_op jit(solution)/shard_map/while/body/eval_jaxpr/ppermute | solution.py:20
  140.6 14.6 %all_gather.9 = bf16[4096,64]{0,1:T(8,128)(2,1)S(1)} all-gather(bf16[1024,64]{0,1:T(8,128)(2,1)S(1)} %collective-permute-done), channel_id=1, replica_groups=mesh['parts'=2,'panel'=4,'zone'=2,'rhs'=2] {'panel'}, dimensions={0}, use_global_device_ids=true | all-gather | bytes 655360 | tf_op jit(solution)/shard_map/while/body/eval_jaxpr/all_gather | solution.py:48
  155.3 6.0 %select_dynamic-update-slice_fusion.2 = (bf16[1024,256]{0,1:T(8,128)(2,1)S(1)}, bf16[1024,64]{0,1:T(8,128)(2,1)S(1)}) fusion(bf16[1024,256]{0,1:T(8,128)(2,1)S(1)} %get-tuple-element.205, s32[]{:T(128)S(6)} %select_n.69, pred[]{:T(512)S(6)} %and.27, bf16[1024,4096]{1,0:T(8,128)(2,1)} %get-tuple-element.220, bf16[4096,64]{0,1:T(8,128)(2,1)S(1)} %all_gather.9, ...), kind=kOutput, calls=%fused_computation.2.clone.1 | convolution fusion | flops 537067520 | bytes 9568261 | tf_op jit(solution)/shard_map/while/body/eval_jaxpr/dot_general | solution.py:46
  161.4 4.4 %collective-permute-start = (bf16[1024,64]{0,1:T(8,128)(2,1)S(1)}, bf16[1024,64]{0,1:T(8,128)(2,1)S(1)}, u32[]{:S(2)}, u32[]{:S(2)}) collective-permute-start(bf16[1024,64]{0,1:T(8,128)(2,1)S(1)} %broadcast_select_fusion.2), channel_id=1, source_target_pairs={{0,2},{1,3},{4,6},{5,7},{8,10},{9,11},{12,14},{13,15},{16,18},{17,... | collective-permute-start | bytes 393224 | tf_op jit(solution)/shard_map/while/body/eval_jaxpr/ppermute | solution.py:20
  165.8 2.5 %collective-permute-done = bf16[1024,64]{0,1:T(8,128)(2,1)S(1)} collective-permute-done((bf16[1024,64]{0,1:T(8,128)(2,1)S(1)}, bf16[1024,64]{0,1:T(8,128)(2,1)S(1)}, u32[]{:S(2)}, u32[]{:S(2)}) %collective-permute-start) | collective-permute-done | bytes 131104 | tf_op jit(solution)/shard_map/while/body/eval_jaxpr/ppermute | solution.py:20
  168.2 14.8 %all_gather.9 = bf16[4096,64]{0,1:T(8,128)(2,1)S(1)} all-gather(bf16[1024,64]{0,1:T(8,128)(2,1)S(1)} %collective-permute-done), channel_id=1, replica_groups=mesh['parts'=2,'panel'=4,'zone'=2,'rhs'=2] {'panel'}, dimensions={0}, use_global_device_ids=true | all-gather | bytes 655360 | tf_op jit(solution)/shard_map/while/body/eval_jaxpr/all_gather | solution.py:48
  183.0 6.0 %select_dynamic-update-slice_fusion.2 = (bf16[1024,256]{0,1:T(8,128)(2,1)S(1)}, bf16[1024,64]{0,1:T(8,128)(2,1)S(1)}) fusion(bf16[1024,256]{0,1:T(8,128)(2,1)S(1)} %get-tuple-element.205, s32[]{:T(128)S(6)} %select_n.69, pred[]{:T(512)S(6)} %and.27, bf16[1024,4096]{1,0:T(8,128)(2,1)} %get-tuple-element.220, bf16[4096,64]{0,1:T(8,128)(2,1)S(1)} %all_gather.9, ...), kind=kOutput, calls=%fused_computation.2.clone.1 | convolution fusion | flops 537067520 | bytes 9568261 | tf_op jit(solution)/shard_map/while/body/eval_jaxpr/dot_general | solution.py:46
  189.1 1.0 copy.4
  (11 shorter events, 0.2 us)
Async XLA Ops:
  0.0 32.3 %copy-start = (bf16[1,1024,256]{2,1,0:T(8,128)(2,1)S(1)}, bf16[1,1024,256]{2,1,0:T(8,128)(2,1)}, u32[]{:S(2)}) copy-start(bf16[1,1024,256]{2,1,0:T(8,128)(2,1)} %param.5) | copy-start | bytes 1572868
  0.0 17.3 %collective-permute-start.1 = (bf16[1024,256]{1,0:T(8,128)(2,1)}, bf16[1024,256]{1,0:T(8,128)(2,1)S(1)}, u32[]{:S(2)}, u32[]{:S(2)}) collective-permute-start(bf16[1024,256]{1,0:T(8,128)(2,1)} %bitcast.19), channel_id=1, source_target_pairs={{0,4},{4,8},{8,12},{12,0},{1,5},{5,9},{9,13},{13,1},{2,6},{6,10},{... | collective-permute-start | bytes 1572872 | tf_op jit(solution)/shard_map/ppermute | solution.py:12
  17.3 14.9 %collective-permute-start.2 = (bf16[1024,256]{1,0:T(8,128)(2,1)S(1)}, bf16[1024,256]{1,0:T(8,128)(2,1)S(1)}, u32[]{:S(2)}, u32[]{:S(2)}) collective-permute-start(bf16[1024,256]{1,0:T(8,128)(2,1)S(1)} %collective-permute-done.1), channel_id=1, source_target_pairs={{0,4},{4,8},{8,12},{12,0},{1,5},{5,9},{9,13},{13,1},{2,6},{6,10},{... | collective-permute-start | bytes 1572872 | tf_op jit(solution)/shard_map/ppermute | solution.py:12
  32.2 14.0 %collective-permute-start.3 = (bf16[1024,256]{1,0:T(8,128)(2,1)S(1)}, bf16[1024,256]{1,0:T(8,128)(2,1)S(1)}, u32[]{:S(2)}, u32[]{:S(2)}) collective-permute-start(bf16[1024,256]{1,0:T(8,128)(2,1)S(1)} %collective-permute-done.2), channel_id=1, source_target_pairs={{0,4},{4,8},{8,12},{12,0},{1,5},{5,9},{9,13},{13,1},{2,6},{6,10},{... | collective-permute-start | bytes 1572872 | tf_op jit(solution)/shard_map/ppermute | solution.py:12
  52.1 5.6 %collective-permute-start = (bf16[1024,64]{0,1:T(8,128)(2,1)S(1)}, bf16[1024,64]{0,1:T(8,128)(2,1)S(1)}, u32[]{:S(2)}, u32[]{:S(2)}) collective-permute-start(bf16[1024,64]{0,1:T(8,128)(2,1)S(1)} %broadcast_select_fusion.2), channel_id=1, source_target_pairs={{0,2},{1,3},{4,6},{5,7},{8,10},{9,11},{12,14},{13,15},{16,18},{17,... | collective-permute-start | bytes 393224 | tf_op jit(solution)/shard_map/while/body/eval_jaxpr/ppermute | solution.py:20
  78.5 6.9 %collective-permute-start = (bf16[1024,64]{0,1:T(8,128)(2,1)S(1)}, bf16[1024,64]{0,1:T(8,128)(2,1)S(1)}, u32[]{:S(2)}, u32[]{:S(2)}) collective-permute-start(bf16[1024,64]{0,1:T(8,128)(2,1)S(1)} %broadcast_select_fusion.2), channel_id=1, source_target_pairs={{0,2},{1,3},{4,6},{5,7},{8,10},{9,11},{12,14},{13,15},{16,18},{17,... | collective-permute-start | bytes 393224 | tf_op jit(solution)/shard_map/while/body/eval_jaxpr/ppermute | solution.py:20
  106.2 6.9 %collective-permute-start = (bf16[1024,64]{0,1:T(8,128)(2,1)S(1)}, bf16[1024,64]{0,1:T(8,128)(2,1)S(1)}, u32[]{:S(2)}, u32[]{:S(2)}) collective-permute-start(bf16[1024,64]{0,1:T(8,128)(2,1)S(1)} %broadcast_select_fusion.2), channel_id=1, source_target_pairs={{0,2},{1,3},{4,6},{5,7},{8,10},{9,11},{12,14},{13,15},{16,18},{17,... | collective-permute-start | bytes 393224 | tf_op jit(solution)/shard_map/while/body/eval_jaxpr/ppermute | solution.py:20
  133.8 6.9 %collective-permute-start = (bf16[1024,64]{0,1:T(8,128)(2,1)S(1)}, bf16[1024,64]{0,1:T(8,128)(2,1)S(1)}, u32[]{:S(2)}, u32[]{:S(2)}) collective-permute-start(bf16[1024,64]{0,1:T(8,128)(2,1)S(1)} %broadcast_select_fusion.2), channel_id=1, source_target_pairs={{0,2},{1,3},{4,6},{5,7},{8,10},{9,11},{12,14},{13,15},{16,18},{17,... | collective-permute-start | bytes 393224 | tf_op jit(solution)/shard_map/while/body/eval_jaxpr/ppermute | solution.py:20
  161.4 6.9 %collective-permute-start = (bf16[1024,64]{0,1:T(8,128)(2,1)S(1)}, bf16[1024,64]{0,1:T(8,128)(2,1)S(1)}, u32[]{:S(2)}, u32[]{:S(2)}) collective-permute-start(bf16[1024,64]{0,1:T(8,128)(2,1)S(1)} %broadcast_select_fusion.2), channel_id=1, source_target_pairs={{0,2},{1,3},{4,6},{5,7},{8,10},{9,11},{12,14},{13,15},{16,18},{17,... | collective-permute-start | bytes 393224 | tf_op jit(solution)/shard_map/while/body/eval_jaxpr/ppermute | solution.py:20
